TPU v7x, 256 devices: a whole 4x4x8 slice. The times are simulated.
256 devices in a mesh: kv: 32 (over z, y), tp: 8 (over x, core).
Axes of the slice: x: 4, y: 4, z: 8, core: 2. Of those that a mesh axis runs over, the one named last changes fastest.
Arguments:
- queries: bfloat16 [8, 4, 128, 128], P(None, None, 'tp'), may hold values from -30 to 30
- cache_keys: bfloat16 [8, 8192, 8, 128], P(None, 'kv', 'tp'), may hold values from -4 to 4
- cache_values: bfloat16 [8, 8192, 8, 128], P(None, 'kv', 'tp'), may hold values from -6 to 6
- new_keys: bfloat16 [8, 4, 8, 128], P(None, None, 'tp'), may hold values from -6 to 6
- new_values: bfloat16 [8, 4, 8, 128], P(None, None, 'tp'), may hold values from -6 to 6
- lengths: int32 [8], replicated, may hold values from 512 to 8192
- residual: bfloat16 [32, 16384], P(None, 'kv'), may hold values from -4 to 4
- out_weight: bfloat16 [16384, 16384], P('tp', 'kv'), may hold values from -0.1875 to 0.1875
- norm_gain: bfloat16 [16384], P('kv'), may hold values from 0.099609375 to 1.8984375
- gate_weight: bfloat16 [16384, 26624], P('kv', 'tp'), may hold values from -0.046875 to 0.046875
- up_weight: bfloat16 [16384, 26624], P('kv', 'tp'), may hold values from -0.046875 to 0.046875
- down_weight: bfloat16 [26624, 16384], P('tp', 'kv'), may hold values from -0.0546875 to 0.0546875
Outputs:
- after_attention: bfloat16 [32, 16384], P(None, 'kv')
- layer_out: bfloat16 [32, 16384], P('tp', 'kv')
All inputs are finite; a program needn't handle non-finite values.
Results may differ from a plain program's by a relative error of at most 0.019.
Values may be sent and summed in bfloat16 or wider, within the bound.
A program may use at most 64 MiB of HBM per device.

v0:
```python
import math
import jax
import jax.numpy as jnp
from jax import lax
from jax.sharding import PartitionSpec as P


def turned_gather(arrays, axis, dims):
    turned = [jnp.moveaxis(a, dim, 0) for a, dim in zip(arrays, dims)]
    both = jnp.concatenate([t.reshape(len(t), -1) for t in turned], axis=1)
    result, at, done = (lax.all_gather(both, axis, axis=0, tiled=True), 0, [])
    for t, dim in zip(turned, dims):
        piece = result[:, at : at + t[0].size].reshape(-1, *t.shape[1:])
        done.append(jnp.moveaxis(piece, 0, dim))
        at += t[0].size
    return tuple(done)


def sent_to_all(array, axis):
    copies = jnp.broadcast_to(array, (lax.axis_size(axis), *array.shape))
    return lax.all_to_all(copies, axis, split_axis=0, concat_axis=0, tiled=True)


def of_everyone(array, axis):
    everything = sent_to_all(array, axis)
    return jnp.sum(everything, axis=0)


def split_up(array, dim, peers):
    before, after = (array.shape[:dim], array.shape[dim + 1 :])
    return jnp.moveaxis(array.reshape(*before, peers, -1, *after), dim, 0)


def summed_on_arrival(array, axis, dim):
    peers = lax.axis_size(axis)
    tiles = lax.all_to_all(split_up(array, dim, peers), axis, 0, 0, tiled=True)
    return jnp.sum(tiles, axis=0)


def side_by_side(arrays, axis, dim, along):
    widths = [a.shape[along] for a in arrays]
    both = jnp.concatenate(arrays, axis=along)
    result = summed_on_arrival(both, axis, dim)
    return tuple(jnp.split(result, [sum(widths[:k]) for k in range(1, len(widths))], axis=along))


def laid_out(tiles, dim):
    dims = list(tiles.shape[1:])
    dims[dim] *= tiles.shape[0]
    return jnp.moveaxis(tiles, 0, dim).reshape(dims)


def collect(array, axis, dim):
    return laid_out(sent_to_all(array, axis), dim)


def fold_sources(received):
    source_max, source_total, source_sum = received
    row_max = jnp.max(source_max, axis=0)
    factor = jnp.exp(source_max - row_max[None])
    return (
        row_max,
        jnp.sum(source_total * factor, axis=0),
        jnp.sum(source_sum * factor[..., None], axis=0),
    )


def local(
    queries,
    cache_keys,
    cache_values,
    new_keys,
    new_values,
    lengths,
    residual,
    out_weight,
    norm_gain,
    gate_weight,
    up_weight,
    down_weight,
):
    seq_count, step_count, heads_local, head_dim = queries.shape
    ctx_local = cache_keys.shape[1]
    kv_local = cache_keys.shape[2]
    group_size = heads_local // kv_local
    scaling = 1.0 / math.sqrt(head_dim)
    grouped = queries.reshape(seq_count, step_count, kv_local, group_size, head_dim)
    scores = (
        jnp.einsum("stgjd,scgd->sgjtc", grouped, cache_keys, preferred_element_type=jnp.float32)
        * scaling
    )
    position = lax.axis_index("kv") * ctx_local + lax.iota(jnp.int32, ctx_local)
    in_range = (position[None, :] < lengths[:, None])[:, None, None, None, :]
    masked = jnp.where(in_range, scores, -1e30)
    local_max = jnp.max(masked, axis=-1)
    weights = jnp.where(in_range, jnp.exp(masked - local_max[..., None]), 0.0)
    local_total = jnp.sum(weights, axis=-1)
    local_sum = jnp.einsum(
        "sgjtc,scgd->sgjtd",
        weights.astype(jnp.bfloat16),
        cache_values,
        preferred_element_type=jnp.float32,
    )
    pieces = lax.axis_size("kv")
    row_max, row_total, row_sum = fold_sources(
        (
            lax.all_to_all(
                local_max.reshape(pieces, -1), "kv", split_axis=0, concat_axis=0, tiled=True
            ),
            lax.all_to_all(
                local_total.reshape(pieces, -1), "kv", split_axis=0, concat_axis=0, tiled=True
            ),
            lax.all_to_all(
                local_sum.reshape(pieces, -1, head_dim),
                "kv",
                split_axis=0,
                concat_axis=0,
                tiled=True,
            ),
        )
    )
    gathered_max, gathered_total, gathered_sum = turned_gather(
        (row_max, row_total, row_sum), "kv", (0, 0, 0)
    )
    cache_max = gathered_max.reshape(local_max.shape)
    cache_total = gathered_total.reshape(local_total.shape)
    cache_sum = gathered_sum.reshape(local_sum.shape)
    fresh_scores = (
        jnp.einsum("stgjd,sugd->sgjtu", grouped, new_keys, preferred_element_type=jnp.float32)
        * scaling
    )
    causal = lax.iota(jnp.int32, step_count)[:, None] >= lax.iota(jnp.int32, step_count)[None, :]
    fresh_scores = jnp.where(causal, fresh_scores, -1e30)
    row_top = jnp.maximum(cache_max, jnp.max(fresh_scores, axis=-1))
    carried = jnp.exp(cache_max - row_top)
    fresh_weights = jnp.where(causal, jnp.exp(fresh_scores - row_top[..., None]), 0.0)
    denominator = cache_total * carried + jnp.sum(fresh_weights, axis=-1)
    numerator = cache_sum * carried[..., None] + jnp.einsum(
        "sgjtu,sugd->sgjtd",
        fresh_weights.astype(jnp.bfloat16),
        new_values,
        preferred_element_type=jnp.float32,
    )
    attended = (
        (numerator / denominator[..., None])
        .transpose(0, 3, 1, 2, 4)
        .reshape(seq_count * step_count, heads_local * head_dim)
        .astype(jnp.bfloat16)
    )
    projected = of_everyone(jnp.dot(attended, out_weight, preferred_element_type=jnp.float32), "tp")
    after_attention = (residual.astype(jnp.float32) + projected).astype(jnp.bfloat16)
    wide_rows = after_attention.astype(jnp.float32)
    model_width = norm_gain.shape[0] * lax.axis_size("kv")
    squares = of_everyone(jnp.sum(wide_rows * wide_rows, axis=1), "kv")
    inverse = lax.rsqrt(squares / model_width + 1e-05)
    normed = (wide_rows * norm_gain.astype(jnp.float32)[None, :] * inverse[:, None]).astype(
        jnp.bfloat16
    )
    gate_part = jnp.dot(normed, gate_weight, preferred_element_type=jnp.float32)
    up_part = jnp.dot(normed, up_weight, preferred_element_type=jnp.float32)
    gate_share, up_share = side_by_side((gate_part, up_part), "kv", 1, 0)
    hidden = collect((jax.nn.silu(gate_share) * up_share).astype(jnp.bfloat16), "kv", 1)
    rows_own = hidden.shape[0] // lax.axis_size("tp")
    own_sums = summed_on_arrival(
        jnp.dot(hidden, down_weight, preferred_element_type=jnp.float32), "tp", 0
    )
    residual_rows = lax.dynamic_slice_in_dim(
        wide_rows, lax.axis_index("tp") * rows_own, rows_own, 0
    )
    return (after_attention, (residual_rows + own_sums).astype(jnp.bfloat16))


def solution(mesh):
    return jax.shard_map(
        local,
        mesh=mesh,
        in_specs=(
            P(None, None, "tp", None),
            P(None, "kv", "tp", None),
            P(None, "kv", "tp", None),
            P(None, None, "tp", None),
            P(None, None, "tp", None),
            P(),
            P(None, "kv"),
            P("tp", "kv"),
            P("kv"),
            P("kv", "tp"),
            P("kv", "tp"),
            P("tp", "kv"),
        ),
        out_specs=(P(None, "kv"), P("tp", "kv")),
        check_vma=False,
    )
```

profile of v0, /device:TPU:1, one launch (start us, length us, event | category | flops | bytes accessed | tf_op | source)
XLA Modules:
  0.0 220.3 jit_solution(5743829172851007249)
XLA Ops:
  2.2 2.2 fusion.37
  5.1 1.5 all_to_all.35
  6.6 12.2 %all-to-all-start = ((f32[32,1,16]{2,1,0:T(1,128)}), f32[32,1,16]{2,1,0:T(1,128)}, u32[]{:S(2)}, u32[]{:S(2)}) async-start(f32[32,1,16]{2,1,0:T(1,128)} %bitcast.93), calls=%async_computation | async-start | bytes 32768 | tf_op jit(solution)/shard_map/all_to_all | solution.py:107
  18.8 1.9 fusion.13
  20.7 1.5 copy.53
  22.1 1.5 all_to_all.37
  23.7 3.5 %all-to-all-done = f32[32,1,16]{2,1,0:T(1,128)} async-done(((f32[32,1,16]{2,1,0:T(1,128)}), f32[32,1,16]{2,1,0:T(1,128)}, u32[]{:S(2)}, u32[]{:S(2)}) %all-to-all-start) | async-done | bytes 2080 | tf_op jit(solution)/shard_map/all_to_all | solution.py:107
  27.2 5.7 %all-to-all-start.1 = ((f32[32,1,16]{2,1,0:T(1,128)}), f32[32,1,16]{2,1,0:T(1,128)}, u32[]{:S(2)}, u32[]{:S(2)}) async-start(f32[32,1,16]{2,1,0:T(1,128)} %bitcast.92), calls=%async_computation.1 | async-start | bytes 32768 | tf_op jit(solution)/shard_map/all_to_all | solution.py:110
  32.9 1.5 fusion.9
  35.2 6.2 %all-to-all-done.1 = f32[32,1,16]{2,1,0:T(1,128)} async-done(((f32[32,1,16]{2,1,0:T(1,128)}), f32[32,1,16]{2,1,0:T(1,128)}, u32[]{:S(2)}, u32[]{:S(2)}) %all-to-all-start.1) | async-done | bytes 2080 | tf_op jit(solution)/shard_map/all_to_all | solution.py:110
  41.5 4.6 %all-to-all-start.2 = ((f32[32,16,128]{2,1,0:T(8,128)}), f32[32,16,128]{2,1,0:T(8,128)}, u32[]{:S(2)}, u32[]{:S(2)}) async-start(f32[32,16,128]{2,1,0:T(8,128)} %bitcast.86), calls=%async_computation.2 | async-start | bytes 524288 | tf_op jit(solution)/shard_map/all_to_all | solution.py:113
  46.6 1.7 fusion.38
  50.0 6.6 %all-to-all-done.2 = f32[32,16,128]{2,1,0:T(8,128)} async-done(((f32[32,16,128]{2,1,0:T(8,128)}), f32[32,16,128]{2,1,0:T(8,128)}, u32[]{:S(2)}, u32[]{:S(2)}) %all-to-all-start.2) | async-done | bytes 262176 | tf_op jit(solution)/shard_map/all_to_all | solution.py:113
  56.6 1.1 multiply_reduce_fusion
  57.8 35.3 %all_gather.3 = f32[512,130]{1,0:T(8,128)S(1)} all-gather(f32[16,130]{1,0:T(8,128)S(1)} %pad_maximum_fusion.1), channel_id=1, replica_groups=mesh['kv'=32,'tp'=8] {'kv'}, dimensions={0}, use_global_device_ids=true | all-gather | bytes 274560 | tf_op jit(solution)/shard_map/all_gather | solution.py:11
  95.7 1.4 fusion.6
  97.1 2.0 fusion.19
  99.2 29.3 %all_to_all.55 = f32[8,32,512]{2,1,0:T(8,128)} all-to-all(f32[8,32,512]{2,1,0:T(8,128)S(1)} %broadcast_in_dim.63), channel_id=1, replica_groups=mesh['kv'=32,'tp'=8] {'tp'}, dimensions={0} | all-to-all | bytes 1048576 | tf_op jit(solution)/shard_map/all_to_all | solution.py:21
  128.5 1.1 reduce_sum.85
  131.0 4.9 %all-to-all-start.4 = ((f32[32,1,32]{2,1,0:T(1,128)}), f32[32,1,32]{2,1,0:T(1,128)S(1)}, u32[]{:S(2)}, u32[]{:S(2)}) async-start(f32[32,1,32]{2,1,0:T(1,128)} %broadcast_in_dim.64), calls=%async_computation.4 | async-start | bytes 32768 | tf_op jit(solution)/shard_map/all_to_all | solution.py:21
  135.9 8.6 %all-to-all-done.4 = f32[32,1,32]{2,1,0:T(1,128)S(1)} async-done(((f32[32,1,32]{2,1,0:T(1,128)}), f32[32,1,32]{2,1,0:T(1,128)S(1)}, u32[]{:S(2)}, u32[]{:S(2)}) %all-to-all-start.4) | async-done | bytes 4128 | tf_op jit(solution)/shard_map/all_to_all | solution.py:21
  145.2 1.2 copy-done.1
  148.2 3.4 %reshape.205 = f32[64,32,104]{2,1,0:T(8,128)} reshape(f32[64,3328]{1,0:T(8,128)} %pad_maximum_fusion) | data formatting | bytes 1703936 | tf_op jit(solution)/shard_map/reshape | solution.py:31
  151.6 1.8 copy.78
  153.4 28.8 %all_to_all.56 = f32[32,64,104]{2,1,0:T(8,128)} all-to-all(f32[32,64,104]{2,1,0:T(8,128)S(1)} %bitcast.85), channel_id=1, replica_groups=mesh['kv'=32,'tp'=8] {'kv'}, dimensions={0} | all-to-all | bytes 1703936 | tf_op jit(solution)/shard_map/all_to_all | solution.py:36
  182.2 1.3 reduce_sum.88
  183.6 17.1 %all_to_all.57 = bf16[32,32,104]{2,1,0:T(8,128)(2,1)S(1)} all-to-all(bf16[32,32,104]{2,1,0:T(8,128)(2,1)S(1)} %broadcast_in_dim.65), channel_id=1, replica_groups=mesh['kv'=32,'tp'=8] {'kv'}, dimensions={0} | all-to-all | bytes 425984 | tf_op jit(solution)/shard_map/all_to_all | solution.py:21
  201.5 2.1 dot_general.33
  203.6 3.3 %fusion = f32[8,4,512]{2,1,0:T(4,128)} fusion(bf16[8,4,3328]{2,1,0:T(4,128)(2,1)} %dot_general.33, bf16[3328,512]{1,0:T(8,128)(2,1)} %param.23), kind=kOutput, calls=%fused_computation | convolution fusion | flops 109051904 | bytes 3686400 | tf_op jit(solution)/shard_map/dot_general | solution.py:165
  207.0 7.1 %all-to-all-start.7 = ((f32[8,4,512]{2,1,0:T(4,128)}), f32[8,4,512]{2,1,0:T(4,128)S(1)}, u32[]{:S(2)}, u32[]{:S(2)}) async-start(f32[8,4,512]{2,1,0:T(4,128)} %fusion), calls=%async_computation.7 | async-start | bytes 131072 | tf_op jit(solution)/shard_map/all_to_all | solution.py:36
  214.1 4.9 %all-to-all-done.7 = f32[8,4,512]{2,1,0:T(4,128)S(1)} async-done(((f32[8,4,512]{2,1,0:T(4,128)}), f32[8,4,512]{2,1,0:T(4,128)S(1)}, u32[]{:S(2)}, u32[]{:S(2)}) %all-to-all-start.7) | async-done | bytes 65568 | tf_op jit(solution)/shard_map/all_to_all | solution.py:36
  219.0 1.3 add_convert_fusion.1
  (48 shorter events, 12.7 us)
Async XLA Ops:
  0.6 143.9 %copy-start = (bf16[512,3328]{1,0:T(8,128)(2,1)S(1)}, bf16[512,3328]{1,0:T(8,128)(2,1)}, u32[]{:S(2)}) copy-start(bf16[512,3328]{1,0:T(8,128)(2,1)} %param.22) | copy-start | bytes 10223620
  0.6 45.9 %copy-start.3 = (bf16[8,4,16,128]{3,2,1,0:T(8,128)(2,1)S(1)}, bf16[8,4,16,128]{3,2,1,0:T(8,128)(2,1)}, u32[]{:S(2)}) copy-start(bf16[8,4,16,128]{3,2,1,0:T(8,128)(2,1)} %param.12) | copy-start | bytes 393220
  1.6 0.6 copy-start.4
  6.6 20.6 %all-to-all-start = ((f32[32,1,16]{2,1,0:T(1,128)}), f32[32,1,16]{2,1,0:T(1,128)}, u32[]{:S(2)}, u32[]{:S(2)}) async-start(f32[32,1,16]{2,1,0:T(1,128)} %bitcast.93), calls=%async_computation | async-start | bytes 32768 | tf_op jit(solution)/shard_map/all_to_all | solution.py:107
  27.2 14.3 %all-to-all-start.1 = ((f32[32,1,16]{2,1,0:T(1,128)}), f32[32,1,16]{2,1,0:T(1,128)}, u32[]{:S(2)}, u32[]{:S(2)}) async-start(f32[32,1,16]{2,1,0:T(1,128)} %bitcast.92), calls=%async_computation.1 | async-start | bytes 32768 | tf_op jit(solution)/shard_map/all_to_all | solution.py:110
  41.5 15.2 %all-to-all-start.2 = ((f32[32,16,128]{2,1,0:T(8,128)}), f32[32,16,128]{2,1,0:T(8,128)}, u32[]{:S(2)}, u32[]{:S(2)}) async-start(f32[32,16,128]{2,1,0:T(8,128)} %bitcast.86), calls=%async_computation.2 | async-start | bytes 524288 | tf_op jit(solution)/shard_map/all_to_all | solution.py:113
  46.1 0.5 copy-start.6
  94.2 35.3 %copy-start.5 = (bf16[32,512]{1,0:T(8,128)(2,1)S(1)}, bf16[32,512]{1,0:T(8,128)(2,1)}, u32[]{:S(2)}) copy-start(bf16[32,512]{1,0:T(8,128)(2,1)} %param.18) | copy-start | bytes 98308
  94.7 41.1 %copy-start.7 = (bf16[512]{0:T(512)(128)(2,1)S(1)}, bf16[512]{0:T(512)(128)(2,1)}, u32[]{:S(2)}) copy-start(bf16[512]{0:T(512)(128)(2,1)} %param.20) | copy-start | bytes 3076
  130.2 16.9 %copy-start.2 = (bf16[32,512]{1,0:T(8,128)(2,1)}, bf16[32,512]{1,0:T(8,128)(2,1)S(1)}, u32[]{:S(2)}) copy-start(bf16[32,512]{1,0:T(8,128)(2,1)S(1)} %get-tuple-element.5) | copy-start | bytes 98308
  131.0 13.5 %all-to-all-start.4 = ((f32[32,1,32]{2,1,0:T(1,128)}), f32[32,1,32]{2,1,0:T(1,128)S(1)}, u32[]{:S(2)}, u32[]{:S(2)}) async-start(f32[32,1,32]{2,1,0:T(1,128)} %broadcast_in_dim.64), calls=%async_computation.4 | async-start | bytes 32768 | tf_op jit(solution)/shard_map/all_to_all | solution.py:21
  144.5 2.0 copy-start.1
  207.0 12.0 %all-to-all-start.7 = ((f32[8,4,512]{2,1,0:T(4,128)}), f32[8,4,512]{2,1,0:T(4,128)S(1)}, u32[]{:S(2)}, u32[]{:S(2)}) async-start(f32[8,4,512]{2,1,0:T(4,128)} %fusion), calls=%async_computation.7 | async-start | bytes 131072 | tf_op jit(solution)/shard_map/all_to_all | solution.py:36
where the time goes:
time: 222 us; the launch traced here: 220 us
  blocking collectives  110 us (50%)
  starting transfers between devices  34.5 us (16%)
  waiting for transfers between devices  29.8 us (13%)
  local copies, waits for them, and re-layouts  19 us (9%)
  matrix products  13.6 us (6%)
  other arithmetic  12.1 us (5%)
    all_to_all x2, blocking collectives, sent_to_all(): return lax.all_to_all(copies, axis, split_axis=0, concat_axis=0, tiled=True)  46.4 us
    all_gather x1, blocking collectives, turned_gather(): result, at, done = (lax.all_gather(both, axis, axis=0, tiled=True), 0, [])  35.3 us
    all_to_all x1, blocking collectives, summed_on_arrival(): tiles = lax.all_to_all(split_up(array, dim, peers), axis, 0, 0, tiled=True)  28.8 us
    all_to_all x1, starting transfers between devices, local(): lax.all_to_all(local_max.reshape(pieces, -1), 'kv', split_axis=0, concat_...  12.2 us
    all_to_all x1, waiting for transfers between devices, sent_to_all(): return lax.all_to_all(copies, axis, split_axis=0, concat_axis=0, tiled=True)  8.6 us
    all_to_all x1, starting transfers between devices, summed_on_arrival(): tiles = lax.all_to_all(split_up(array, dim, peers), axis, 0, 0, tiled=True)  7.12 us
    all_to_all x1, waiting for transfers between devices, local(): lax.all_to_all(local_sum.reshape(pieces, -1, head_dim), 'kv', split_axis=...  6.58 us
    all_to_all x1, waiting for transfers between devices, local(): lax.all_to_all(local_total.reshape(pieces, -1), 'kv', split_axis=0, conca...  6.2 us
  transfers between devices with their start and end apart: 5, of which 5 were waited for; matrix products, arithmetic and copies ran while one was open for 4% of the time, Pallas kernels for 0%

commit v1 on v0

--- a/solution.py
+++ b/solution.py
@@ -8,7 +8,13 @@
 def turned_gather(arrays, axis, dims):
     turned = [jnp.moveaxis(a, dim, 0) for a, dim in zip(arrays, dims)]
     both = jnp.concatenate([t.reshape(len(t), -1) for t in turned], axis=1)
-    result, at, done = (lax.all_gather(both, axis, axis=0, tiled=True), 0, [])
+    result, at, done = (
+        jnp.concatenate(
+            lax.all_to_all(jnp.stack([both] * lax.axis_size(axis)), axis, 0, 0), axis=0
+        ),
+        0,
+        [],
+    )
     for t, dim in zip(turned, dims):
         piece = result[:, at : at + t[0].size].reshape(-1, *t.shape[1:])
         done.append(jnp.moveaxis(piece, 0, dim))

time: 222 us -> 197 us (0.89)
  blocking collectives: 110 us -> 65.2 us
  waiting for transfers between devices: 29.8 us -> 40.5 us
  local copies, waits for them, and re-layouts: 19 us -> 23.8 us
  starting transfers between devices: 34.5 us -> 38.3 us
    all_gather x1 -> x0, blocking collectives: 35.3 us -> none  [turned_gather(): result, at, done = (lax.all_gather(both, axis, axis=0, tiled=True), 0, [])]
    all_to_all x0 -> x1, waiting for transfers between devices: none -> 10.8 us  [turned_gather(): lax.all_to_all(jnp.stack([both] * lax.axis_size(axis)), axis, 0, 0)]
    all_to_all x2, blocking collectives: 46.4 us -> 36.4 us  [sent_to_all(): return lax.all_to_all(copies, axis, split_axis=0, concat_axis=0, tiled=True)]
    all_to_all x0 -> x1, starting transfers between devices: none -> 4.61 us  [turned_gather(): lax.all_to_all(jnp.stack([both] * lax.axis_size(axis)), axis, 0, 0)]
  transfers between devices with their start and end apart: 5 -> 6, of which waited for: 5 -> 6; matrix products, arithmetic and copies ran while one was open for 4% -> 6% of each run, Pallas kernels for 0% -> 0%
where the time goes in v1:
time: 197 us; the launch traced here: 196 us
  blocking collectives  65.2 us (33%)
  waiting for transfers between devices  40.5 us (21%)
  starting transfers between devices  38.3 us (19%)
  local copies, waits for them, and re-layouts  23.8 us (12%)
  matrix products  13.6 us (7%)
  other arithmetic  13.4 us (7%)
    all_to_all x2, blocking collectives, sent_to_all(): return lax.all_to_all(copies, axis, split_axis=0, concat_axis=0, tiled=True)  36.4 us
    all_to_all x1, blocking collectives, summed_on_arrival(): tiles = lax.all_to_all(split_up(array, dim, peers), axis, 0, 0, tiled=True)  28.8 us
    all_to_all x1, starting transfers between devices, local(): lax.all_to_all(local_max.reshape(pieces, -1), 'kv', split_axis=0, concat_...  12.2 us
    all_to_all x1, waiting for transfers between devices, turned_gather(): lax.all_to_all(jnp.stack([both] * lax.axis_size(axis)), axis, 0, 0)  10.8 us
    all_to_all x1, waiting for transfers between devices, sent_to_all(): return lax.all_to_all(copies, axis, split_axis=0, concat_axis=0, tiled=True)  8.6 us
    all_to_all x1, starting transfers between devices, summed_on_arrival(): tiles = lax.all_to_all(split_up(array, dim, peers), axis, 0, 0, tiled=True)  7.11 us
    all_to_all x1, waiting for transfers between devices, local(): lax.all_to_all(local_sum.reshape(pieces, -1, head_dim), 'kv', split_axis=...  6.42 us
    all_to_all x1, waiting for transfers between devices, local(): lax.all_to_all(local_total.reshape(pieces, -1), 'kv', split_axis=0, conca...  6.2 us
  transfers between devices with their start and end apart: 6, of which 6 were waited for; matrix products, arithmetic and copies ran while one was open for 6% of the time, Pallas kernels for 0%

profile of v1, /device:TPU:1, one launch (start us, length us, event | category | flops | bytes accessed | tf_op | source)
XLA Modules:
  0.0 195.6 jit_solution(7530040644546533926)
XLA Ops:
  2.2 2.2 %fusion.37 = (f32[8,16,4]{1,2,0:T(4,128)S(1)}, f32[8,1,16,4,256]{4,2,3,0,1:T(8,128)}) fusion(bf16[8,4,16,128]{3,2,1,0:T(8,128)(2,1)} %param.12, bf16[8,256,1,128]{3,1,2,0:T(8,128)(2,1)} %param.13, pred[8,256]{1,0:T(8,128)(4,1)S(1)} %broadcast_compare_fusion), kind=kOutput, calls=%fused_computation.60 | convolution fusion | flops 33947136 | bytes 1183744 | tf_op jit(solution)/shard_map/stgjd,scgd->sgjtc/dot_general | solution.py:95
  5.1 1.5 all_to_all.38
  6.6 12.2 %all-to-all-start = ((f32[32,1,16]{2,1,0:T(1,128)}), f32[32,1,16]{2,1,0:T(1,128)}, u32[]{:S(2)}, u32[]{:S(2)}) async-start(f32[32,1,16]{2,1,0:T(1,128)} %bitcast.94), calls=%async_computation | async-start | bytes 32768 | tf_op jit(solution)/shard_map/all_to_all | solution.py:113
  18.8 1.9 fusion.13
  20.7 1.5 copy.53
  22.1 1.5 all_to_all.40
  23.7 3.5 %all-to-all-done = f32[32,1,16]{2,1,0:T(1,128)} async-done(((f32[32,1,16]{2,1,0:T(1,128)}), f32[32,1,16]{2,1,0:T(1,128)}, u32[]{:S(2)}, u32[]{:S(2)}) %all-to-all-start) | async-done | bytes 2080 | tf_op jit(solution)/shard_map/all_to_all | solution.py:113
  27.2 5.7 %all-to-all-start.1 = ((f32[32,1,16]{2,1,0:T(1,128)}), f32[32,1,16]{2,1,0:T(1,128)}, u32[]{:S(2)}, u32[]{:S(2)}) async-start(f32[32,1,16]{2,1,0:T(1,128)} %bitcast.93), calls=%async_computation.1 | async-start | bytes 32768 | tf_op jit(solution)/shard_map/all_to_all | solution.py:116
  32.9 1.5 fusion.9
  35.2 6.2 %all-to-all-done.1 = f32[32,1,16]{2,1,0:T(1,128)} async-done(((f32[32,1,16]{2,1,0:T(1,128)}), f32[32,1,16]{2,1,0:T(1,128)}, u32[]{:S(2)}, u32[]{:S(2)}) %all-to-all-start.1) | async-done | bytes 2080 | tf_op jit(solution)/shard_map/all_to_all | solution.py:116
  41.5 4.6 %all-to-all-start.2 = ((f32[32,16,128]{2,1,0:T(8,128)}), f32[32,16,128]{2,1,0:T(8,128)}, u32[]{:S(2)}, u32[]{:S(2)}) async-start(f32[32,16,128]{2,1,0:T(8,128)} %bitcast.87), calls=%async_computation.2 | async-start | bytes 524288 | tf_op jit(solution)/shard_map/all_to_all | solution.py:119
  47.5 1.3 multiply_reduce_fusion.2
  48.8 1.3 copy.57
  50.2 6.4 %all-to-all-done.2 = f32[32,16,128]{2,1,0:T(8,128)} async-done(((f32[32,16,128]{2,1,0:T(8,128)}), f32[32,16,128]{2,1,0:T(8,128)}, u32[]{:S(2)}, u32[]{:S(2)}) %all-to-all-start.2) | async-done | bytes 262176 | tf_op jit(solution)/shard_map/all_to_all | solution.py:119
  59.4 4.6 %all-to-all-start.3 = ((f32[32,16,130]{2,1,0:T(8,128)}), f32[32,16,130]{2,1,0:T(8,128)}, u32[]{:S(2)}, u32[]{:S(2)}) async-start(f32[32,16,130]{2,1,0:T(8,128)} %stack.2), calls=%async_computation.3 | async-start | bytes 1048576 | tf_op jit(solution)/shard_map/all_to_all | solution.py:13
  64.5 1.7 fusion.38
  66.3 10.8 %all-to-all-done.3 = f32[32,16,130]{2,1,0:T(8,128)} async-done(((f32[32,16,130]{2,1,0:T(8,128)}), f32[32,16,130]{2,1,0:T(8,128)}, u32[]{:S(2)}, u32[]{:S(2)}) %all-to-all-start.3) | async-done | bytes 266272 | tf_op jit(solution)/shard_map/all_to_all | solution.py:13
  77.1 1.3 slice_reduce_fusion
  78.4 1.9 slice.12
  81.8 1.4 fusion.6
  83.2 2.0 %fusion.19 = f32[32,512]{1,0:T(8,128)S(1)} fusion(bf16[2048,512]{1,0:T(8,128)(2,1)} %param.19, bf16[4,8,16,128]{3,2,1,0:T(8,128)(2,1)S(1)} %bitcast.92), kind=kOutput, calls=%fused_computation.28 | convolution fusion | flops 67108864 | bytes 2293760 | tf_op jit(solution)/shard_map/dot_general | solution.py:156
  85.3 19.3 %all_to_all.60 = f32[8,32,512]{2,1,0:T(8,128)} all-to-all(f32[8,32,512]{2,1,0:T(8,128)S(1)} %broadcast_in_dim.63), channel_id=1, replica_groups=mesh['kv'=32,'tp'=8] {'tp'}, dimensions={0} | all-to-all | bytes 1048576 | tf_op jit(solution)/shard_map/all_to_all | solution.py:27
  107.1 4.1 %all-to-all-start.5 = ((f32[32,1,32]{2,1,0:T(1,128)}), f32[32,1,32]{2,1,0:T(1,128)S(1)}, u32[]{:S(2)}, u32[]{:S(2)}) async-start(f32[32,1,32]{2,1,0:T(1,128)} %broadcast_in_dim.64), calls=%async_computation.5 | async-start | bytes 32768 | tf_op jit(solution)/shard_map/all_to_all | solution.py:27
  111.2 8.6 %all-to-all-done.5 = f32[32,1,32]{2,1,0:T(1,128)S(1)} async-done(((f32[32,1,32]{2,1,0:T(1,128)}), f32[32,1,32]{2,1,0:T(1,128)S(1)}, u32[]{:S(2)}, u32[]{:S(2)}) %all-to-all-start.5) | async-done | bytes 4128 | tf_op jit(solution)/shard_map/all_to_all | solution.py:27
  123.5 3.4 %reshape.211 = f32[64,32,104]{2,1,0:T(8,128)} reshape(f32[64,3328]{1,0:T(8,128)} %pad_maximum_fusion) | data formatting | bytes 1703936 | tf_op jit(solution)/shard_map/reshape | solution.py:37
  126.9 1.8 copy.78
  128.8 28.8 %all_to_all.61 = f32[32,64,104]{2,1,0:T(8,128)} all-to-all(f32[32,64,104]{2,1,0:T(8,128)S(1)} %bitcast.86), channel_id=1, replica_groups=mesh['kv'=32,'tp'=8] {'kv'}, dimensions={0} | all-to-all | bytes 1703936 | tf_op jit(solution)/shard_map/all_to_all | solution.py:42
  158.9 17.1 %all_to_all.62 = bf16[32,32,104]{2,1,0:T(8,128)(2,1)S(1)} all-to-all(bf16[32,32,104]{2,1,0:T(8,128)(2,1)S(1)} %broadcast_in_dim.65), channel_id=1, replica_groups=mesh['kv'=32,'tp'=8] {'kv'}, dimensions={0} | all-to-all | bytes 425984 | tf_op jit(solution)/shard_map/all_to_all | solution.py:27
  176.8 2.1 %dot_general.33 = bf16[8,4,3328]{2,1,0:T(4,128)(2,1)} reshape(bf16[32,32,104]{2,1,0:T(8,128)(2,1)} %copy.64) | data formatting | bytes 425984 | tf_op jit(solution)/shard_map/dot_general | solution.py:171
  179.0 3.4 %fusion = f32[8,4,512]{2,1,0:T(4,128)} fusion(bf16[8,4,3328]{2,1,0:T(4,128)(2,1)} %dot_general.33, bf16[3328,512]{1,0:T(8,128)(2,1)} %param.23), kind=kOutput, calls=%fused_computation | convolution fusion | flops 109051904 | bytes 3686400 | tf_op jit(solution)/shard_map/dot_general | solution.py:171
  182.3 7.1 %all-to-all-start.8 = ((f32[8,4,512]{2,1,0:T(4,128)}), f32[8,4,512]{2,1,0:T(4,128)S(1)}, u32[]{:S(2)}, u32[]{:S(2)}) async-start(f32[8,4,512]{2,1,0:T(4,128)} %fusion), calls=%async_computation.8 | async-start | bytes 131072 | tf_op jit(solution)/shard_map/all_to_all | solution.py:42
  189.4 4.9 %all-to-all-done.8 = f32[8,4,512]{2,1,0:T(4,128)S(1)} async-done(((f32[8,4,512]{2,1,0:T(4,128)}), f32[8,4,512]{2,1,0:T(4,128)S(1)}, u32[]{:S(2)}, u32[]{:S(2)}) %all-to-all-start.8) | async-done | bytes 65568 | tf_op jit(solution)/shard_map/all_to_all | solution.py:42
  (52 shorter events, 18.9 us)
Async XLA Ops:
  0.6 119.2 %copy-start = (bf16[512,3328]{1,0:T(8,128)(2,1)S(1)}, bf16[512,3328]{1,0:T(8,128)(2,1)}, u32[]{:S(2)}) copy-start(bf16[512,3328]{1,0:T(8,128)(2,1)} %param.22) | copy-start | bytes 10223620
  0.6 63.9 %copy-start.3 = (bf16[8,4,16,128]{3,2,1,0:T(8,128)(2,1)S(1)}, bf16[8,4,16,128]{3,2,1,0:T(8,128)(2,1)}, u32[]{:S(2)}) copy-start(bf16[8,4,16,128]{3,2,1,0:T(8,128)(2,1)} %param.12) | copy-start | bytes 393220
  1.6 0.6 copy-start.4
  6.6 20.6 %all-to-all-start = ((f32[32,1,16]{2,1,0:T(1,128)}), f32[32,1,16]{2,1,0:T(1,128)}, u32[]{:S(2)}, u32[]{:S(2)}) async-start(f32[32,1,16]{2,1,0:T(1,128)} %bitcast.94), calls=%async_computation | async-start | bytes 32768 | tf_op jit(solution)/shard_map/all_to_all | solution.py:113
  27.2 14.3 %all-to-all-start.1 = ((f32[32,1,16]{2,1,0:T(1,128)}), f32[32,1,16]{2,1,0:T(1,128)}, u32[]{:S(2)}, u32[]{:S(2)}) async-start(f32[32,1,16]{2,1,0:T(1,128)} %bitcast.93), calls=%async_computation.1 | async-start | bytes 32768 | tf_op jit(solution)/shard_map/all_to_all | solution.py:116
  41.5 15.2 %all-to-all-start.2 = ((f32[32,16,128]{2,1,0:T(8,128)}), f32[32,16,128]{2,1,0:T(8,128)}, u32[]{:S(2)}, u32[]{:S(2)}) async-start(f32[32,16,128]{2,1,0:T(8,128)} %bitcast.87), calls=%async_computation.2 | async-start | bytes 524288 | tf_op jit(solution)/shard_map/all_to_all | solution.py:119
  46.8 0.7 copy-start.6
  59.4 17.7 %all-to-all-start.3 = ((f32[32,16,130]{2,1,0:T(8,128)}), f32[32,16,130]{2,1,0:T(8,128)}, u32[]{:S(2)}, u32[]{:S(2)}) async-start(f32[32,16,130]{2,1,0:T(8,128)} %stack.2), calls=%async_computation.3 | async-start | bytes 1048576 | tf_op jit(solution)/shard_map/all_to_all | solution.py:13
  64.0 0.5 copy-start.7
  80.3 25.4 %copy-start.5 = (bf16[32,512]{1,0:T(8,128)(2,1)S(1)}, bf16[32,512]{1,0:T(8,128)(2,1)}, u32[]{:S(2)}) copy-start(bf16[32,512]{1,0:T(8,128)(2,1)} %param.18) | copy-start | bytes 98308
  80.8 30.4 %copy-start.8 = (bf16[512]{0:T(512)(128)(2,1)S(1)}, bf16[512]{0:T(512)(128)(2,1)}, u32[]{:S(2)}) copy-start(bf16[512]{0:T(512)(128)(2,1)} %param.20) | copy-start | bytes 3076
  106.3 16.2 %copy-start.2 = (bf16[32,512]{1,0:T(8,128)(2,1)}, bf16[32,512]{1,0:T(8,128)(2,1)S(1)}, u32[]{:S(2)}) copy-start(bf16[32,512]{1,0:T(8,128)(2,1)S(1)} %get-tuple-element.5) | copy-start | bytes 98308
  107.1 12.8 %all-to-all-start.5 = ((f32[32,1,32]{2,1,0:T(1,128)}), f32[32,1,32]{2,1,0:T(1,128)S(1)}, u32[]{:S(2)}, u32[]{:S(2)}) async-start(f32[32,1,32]{2,1,0:T(1,128)} %broadcast_in_dim.64), calls=%async_computation.5 | async-start | bytes 32768 | tf_op jit(solution)/shard_map/all_to_all | solution.py:27
  119.8 2.0 %copy-start.1 = (bf16[512,3328]{1,0:T(8,128)(2,1)S(1)}, bf16[512,3328]{1,0:T(8,128)(2,1)}, u32[]{:S(2)}) copy-start(bf16[512,3328]{1,0:T(8,128)(2,1)} %param.21) | copy-start | bytes 10223620
  182.3 12.0 %all-to-all-start.8 = ((f32[8,4,512]{2,1,0:T(4,128)}), f32[8,4,512]{2,1,0:T(4,128)S(1)}, u32[]{:S(2)}, u32[]{:S(2)}) async-start(f32[8,4,512]{2,1,0:T(4,128)} %fusion), calls=%async_computation.8 | async-start | bytes 131072 | tf_op jit(solution)/shard_map/all_to_all | solution.py:42
